TPU v7x, 128 devices: a whole 4x4x4 slice. The times are simulated.
128 devices in a mesh: user: 8 (over y, core), item: 16 (over x, z).
Axes of the slice: x: 4, y: 4, z: 4, core: 2. Of those that a mesh axis runs over, the one named last changes fastest.
Arguments:
- item_factor: float32 [32768, 256], P(('item', 'user')), may hold values from -36 to 36
- context_factor: float32 [4096, 256], replicated, may hold values from -6 to 6
- tile_count: int32 [8, 16], P('user', 'item'), may hold values from 16 to 128, as said below
- tile_rows: int32 [8, 16, 128], P('user', 'item'), may hold values from 0 to 63
- tile_cols: int32 [8, 16, 128], P('user', 'item'), may hold values from 0 to 31
- tile_ctx: int32 [8, 16, 128], P('user', 'item'), may hold values from 0 to 63
- nz_offsets: int32 [8, 16, 3, 128, 512], P('user', 'item'), may hold values from 0 to 63
- nz_values: float32 [8, 16, 128, 512], P('user', 'item'), may hold values from -6 to 6
Outputs:
- user_factor: float32 [32768, 256], P(('user', 'item'))
- new_items: float32 [32768, 256], P(('item', 'user'))
Inputs may be any that keep to these rules, and one draw needn't show every extreme that they name: `tile_count`: some device has all 128 tiles live; the others 128, half, a quarter or an eighth of them.
All inputs are finite; a program needn't handle non-finite values.
Results may differ from a plain program's by a relative error of at most 0.0066.
Values may be sent and summed in bfloat16 or wider, within the bound.
A program may use at most 128 MiB of HBM per device.

v0:
```python
import functools
import math

import jax
import jax.numpy as jnp
from jax import lax
from jax.experimental import pallas as pl
from jax.experimental.pallas import tpu as pltpu
from jax.sharding import PartitionSpec as P

TILE = 64
UNROLL = 32
PLAN = (3, 2)
PAIR = 2 * TILE
BLOCK = 64
SPLIT = 2
HOPS = (1, 3, 2)
PIVOTS = 4
HIGHEST = lax.Precision.HIGHEST
MESH = pl.DeviceIdType.MESH
VMEM_SPEC = pl.BlockSpec(memory_space=pltpu.VMEM)
SMEM_SPEC = pl.BlockSpec(memory_space=pltpu.SMEM)


def dot(left, right):
    return jnp.dot(left, right, precision=HIGHEST, preferred_element_type=jnp.float32)


def gram_of(columns):
    return lax.dot_general(
        columns,
        columns,
        (((1,), (1,)), ((), ())),
        precision=HIGHEST,
        preferred_element_type=jnp.float32,
    )


def mttkrp_kernel(
    target_at,
    count,
    target_ids,
    source_ids,
    context_ids,
    offsets,
    values,
    source,
    context,
    out,
    totals,
):
    totals[...] = jnp.zeros_like(totals)
    rank, entries = totals.shape[2], offsets.shape[2]

    def one_hot(row, extent):
        positions = lax.broadcasted_iota(jnp.int32, (extent, entries), 0)
        return jnp.where(positions == row, 1.0, 0.0).astype(jnp.bfloat16)

    def lanes_of(pair, row):
        wide = pair.astype(jnp.float32)
        picked = [
            jnp.take_along_axis(
                wide,
                jnp.broadcast_to(row[:, at : at + PAIR], (rank, PAIR)),
                axis=1,
                mode="promise_in_bounds",
            )
            for at in range(0, entries, PAIR)
        ]
        return jnp.concatenate(picked, axis=1)

    def group(step, carry):
        first = pl.multiple_of(step * UNROLL, UNROLL)
        targets = offsets[target_at, pl.ds(first, UNROLL), :]
        sources = offsets[1 - target_at, pl.ds(first, UNROLL), :]
        contexts = offsets[2, pl.ds(first, UNROLL), :]
        weights = values[pl.ds(first, UNROLL), :]
        for at in range(UNROLL):
            row = slice(at, at + 1)
            source_id, context_id = source_ids[first + at], context_ids[first + at]
            source_row = sources[row] + TILE * lax.rem(source_id, 2)
            context_row = contexts[row] + TILE * lax.rem(context_id, 2)
            source_part = jnp.dot(
                source[lax.div(source_id, 2)],
                one_hot(source_row, PAIR),
                preferred_element_type=jnp.float32,
            )
            context_part = lanes_of(context[lax.div(context_id, 2)], context_row)
            weight = jnp.where(first + at < count[0], weights[row], 0.0)
            terms = (weight * source_part * context_part).astype(jnp.bfloat16)
            totals[target_ids[first + at]] += lax.dot_general(
                one_hot(targets[row], TILE),
                terms,
                (((1,), (1,)), ((), ())),
                preferred_element_type=jnp.float32,
            )
        return carry

    lax.fori_loop(0, (count[0] + UNROLL - 1) // UNROLL, group, 0)
    out[...] = totals[...].astype(out.dtype)


def mttkrp(target_at, count, ids, offsets, values, source_pairs, context_pairs, tiles):
    shape = (tiles, TILE, source_pairs.shape[1])
    return pl.pallas_call(
        functools.partial(mttkrp_kernel, target_at),
        out_shape=jax.ShapeDtypeStruct(shape, jnp.bfloat16),
        in_specs=[SMEM_SPEC] * 4 + [VMEM_SPEC] * 4,
        out_specs=VMEM_SPEC,
        scratch_shapes=[pltpu.VMEM(shape, jnp.float32)],
        compiler_params=pltpu.CompilerParams(vmem_limit_bytes=24 * 2**20),
        name="mttkrp",
    )(
        count,
        ids[target_at],
        ids[1 - target_at],
        ids[2],
        offsets,
        values,
        source_pairs,
        context_pairs,
    )


def greet(groups):
    barrier = pltpu.get_barrier_semaphore()
    for axis, size in groups:
        me = lax.axis_index(axis)
        for ahead in range(1, size):
            pl.semaphore_signal(
                barrier, inc=1, device_id={axis: lax.rem(me + ahead, size)}, device_id_type=MESH
            )


def await_greetings(groups):
    pl.semaphore_wait(pltpu.get_barrier_semaphore(), sum(size - 1 for _, size in groups))


def send_all(axis, size, source, target, sems):
    me = lax.axis_index(axis)
    copies = []
    for ahead in range(1, size):
        peer = lax.rem(me + ahead, size)
        copy = pltpu.make_async_remote_copy(
            src_ref=source(peer, ahead),
            dst_ref=target(me, ahead),
            send_sem=sems.at[0, ahead - 1],
            recv_sem=sems.at[1, ahead - 1],
            device_id={axis: peer},
            device_id_type=MESH,
        )
        copy.start()
        copies.append(copy)
    return copies


def copy_to(source, target, sems, user, item):
    copy = pltpu.make_async_remote_copy(
        src_ref=source,
        dst_ref=target,
        send_sem=sems.at[0],
        recv_sem=sems.at[1],
        device_id=(user, item),
        device_id_type=MESH,
    )
    copy.start()
    return copy


def receive(copies):
    for copy in copies:
        copy.wait_recv()


def rows_of(item, rows):
    return pl.ds(pl.multiple_of(item * rows, rows), rows)


def gram_to_users(gram, by_user, sems, users):
    rows = by_user.shape[1]
    user = lax.axis_index("user")
    by_user[user] = gram[rows_of(user, rows), :]
    return send_all(
        "user",
        users,
        lambda peer, ahead: gram.at[rows_of(peer, rows)],
        lambda me, ahead: by_user.at[me],
        sems,
    )


def torus(side):
    item = lax.axis_index("item")
    slow, fast = item // side, lax.rem(item, side)

    def at_slow(ahead):
        return lax.rem(slow + ahead, side) * side + fast

    def at_fast(ahead):
        return slow * side + lax.rem(fast + ahead, side)

    return slow, fast, at_slow, at_fast


def exchange(before, terms, place, along, spread, sems):
    receive(before)
    spread[place] = jnp.sum(terms[...], axis=0)
    user = lax.axis_index("user")
    return [
        copy_to(spread.at[place], spread.at[place], sems.at[ahead - 1], user, along(ahead))
        for ahead in HOPS
    ]


def blocks_back(block, result, sems, users):
    rows = block.shape[0]
    span = rows_of(lax.axis_index("user"), rows)
    result[span, :] = block[...]
    return send_all("user", users, lambda peer, ahead: block, lambda me, ahead: result.at[span], sems)


def gram_scratch(users, side, width):
    rows = width // users
    return [
        pltpu.VMEM((width, width), jnp.float32),
        pltpu.VMEM((users, rows, width), jnp.float32),
        pltpu.VMEM((side, rows, width), jnp.float32),
        pltpu.VMEM((side, rows, width), jnp.float32),
        pltpu.SemaphoreType.DMA((2, users - 1)),
        pltpu.SemaphoreType.DMA((side - 1, 2)),
        pltpu.SemaphoreType.DMA((side - 1, 2)),
    ]


def small_inverse(matrix):
    size = len(matrix)
    if size == 2:
        (first, off), (_, last) = matrix
        scale = 1.0 / (first * last - off * off)
        cross = -off * scale
        return [[last * scale, cross], [cross, first * scale]]
    half = size // 2

    def product(left, right):
        return [
            [sum(left[i][k] * right[k][j] for k in range(1, half)) + left[i][0] * right[0][j] for j in range(half)]
            for i in range(half)
        ]

    corner = small_inverse([row[:half] for row in matrix[:half]])
    side = [row[half:] for row in matrix[:half]]
    solved = product(corner, side)
    lowered = product([list(column) for column in zip(*side)], solved)
    rest = small_inverse(
        [[matrix[half + i][half + j] - lowered[i][j] for j in range(half)] for i in range(half)]
    )
    spread = product(solved, rest)
    update = product(spread, [list(column) for column in zip(*solved)])
    top = [
        [corner[i][j] + update[i][j] for j in range(half)] + [-spread[i][j] for j in range(half)]
        for i in range(half)
    ]
    bottom = [[-spread[j][i] for j in range(half)] + rest[i] for i in range(half)]
    return top + bottom


def invert(work, first_block, last_block):
    width = work.shape[0]
    down = lax.broadcasted_iota(jnp.int32, (BLOCK, BLOCK), 0)
    across = lax.broadcasted_iota(jnp.int32, (BLOCK, BLOCK), 1)
    lanes = lax.broadcasted_iota(jnp.int32, (BLOCK, width), 1) // BLOCK
    rows = lax.broadcasted_iota(jnp.int32, (width, BLOCK), 0) // BLOCK
    full_lanes = lax.broadcasted_iota(jnp.int32, (width, width), 1) // BLOCK
    steps = range(PIVOTS)
    for block in range(first_block, last_block):
        span = slice(block * BLOCK, (block + 1) * BLOCK)
        pivot = work[span, span]
        for at in range(0, BLOCK, PIVOTS):
            columns = [
                jnp.broadcast_to(pivot[:, at + i : at + i + 1], (BLOCK, BLOCK)) for i in steps
            ]
            inverse = small_inverse(
                [
                    [columns[max(i, j)][at + min(i, j) : at + min(i, j) + 1, :] for j in steps]
                    for i in steps
                ]
            )
            fresh = []
            for i in steps:
                row = inverse[i][0] * pivot[at : at + 1, :]
                for j in steps[1:]:
                    row = row + inverse[i][j] * pivot[at + j : at + j + 1, :]
                for j in steps:
                    row = jnp.where(across[:1] == at + j, inverse[i][j], row)
                fresh.append(row)
            after = jnp.where((across >= at) & (across < at + PIVOTS), 0.0, pivot)
            for i in steps:
                after = after - columns[i] * fresh[i]
            for i in steps:
                after = jnp.where(down == at + i, fresh[i], after)
            pivot = after
        panel = dot(pivot, work[span, :])
        panel = jnp.where(lanes == block, jnp.concatenate([pivot] * (width // BLOCK), axis=1), panel)
        column = jnp.where(rows == block, 0.0, work[:, span])
        kept = jnp.where(full_lanes == block, 0.0, work[...])
        work[...] = kept - dot(column, panel)
        work[span, :] = panel


def gather_kernel(
    axis_sizes, side, step_rows, item_factor, context_factor, items, context, gram_rows, context_gram,
    own_rows, loaded, load_sems, own_sems, sibling_sems,
    gram, by_user, by_slow, by_fast, user_sems, slow_sems, fast_sems,
):
    users, items_extent = axis_sizes
    everyone = (("user", users), ("item", items_extent))
    user, item = lax.axis_index("user"), lax.axis_index("item")
    slow, fast, at_slow, at_fast = torus(side)
    steps = context_factor.shape[0] // step_rows
    pairs = step_rows // PAIR
    greet(everyone)

    def load(step):
        span = pl.ds(pl.multiple_of(step * step_rows, step_rows), step_rows)
        return pltpu.make_async_copy(context_factor.at[span], loaded.at[step], load_sems.at[step])

    def transform(step, carry):
        load(step).wait()
        chunk = loaded[step]
        columns = chunk.T
        for pair in range(pairs):
            context[step * pairs + pair] = columns[:, pair * PAIR : (pair + 1) * PAIR].astype(
                jnp.bfloat16
            )
        context_gram[...] += gram_of(columns)
        return carry

    fetch = pltpu.make_async_copy(item_factor, own_rows, load_sems.at[steps])
    fetch.start()
    for step in range(steps):
        load(step).start()
    context_gram[...] = jnp.zeros_like(context_gram)
    fetch.wait()
    columns = own_rows[...].T
    for pair in range(items.shape[1]):
        items[user, pair] = columns[:, pair * PAIR : (pair + 1) * PAIR].astype(jnp.bfloat16)
    gram[...] = gram_of(columns)
    await_greetings(everyone)
    first = gram_to_users(gram, by_user, user_sems, users)
    core = lax.rem(user, 2)
    sibling = user + 1 - 2 * core
    own = []
    for ahead in HOPS:
        peer = lax.rem(user + 2 * ahead, users)
        own.append(copy_to(items.at[user], items.at[user], own_sems.at[ahead - 1], peer, item))
    forwarded = [copy_to(items.at[user], items.at[user], sibling_sems.at[0], sibling, item)]

    def forward(at):
        own[at].wait_recv()
        block = items.at[lax.rem(user + users - 2 * HOPS[at], users)]
        forwarded.append(copy_to(block, block, sibling_sems.at[1 + at], sibling, item))

    lax.fori_loop(0, PLAN[0], transform, 0)
    second = exchange(first, by_user, slow, at_slow, by_slow, slow_sems)
    forward(0)
    forward(1)
    lax.fori_loop(PLAN[0], PLAN[0] + PLAN[1], transform, 0)
    third = exchange(second, by_slow, fast, at_fast, by_fast, fast_sems)
    forward(2)
    lax.fori_loop(PLAN[0] + PLAN[1], steps, transform, 0)
    receive(third)
    gram_rows[...] = jnp.sum(by_fast[...], axis=0)
    receive(forwarded)
    for copy in first + own + forwarded + second + third:
        copy.wait_send()


def gather_items(item_factor, context_factor, axis_sizes, side):
    users, items = axis_sizes
    rows, width = item_factor.shape
    contexts = context_factor.shape[0]
    step_rows = 512
    return pl.pallas_call(
        functools.partial(gather_kernel, axis_sizes, side, step_rows),
        out_shape=(
            jax.ShapeDtypeStruct((users, rows // PAIR, width, PAIR), jnp.bfloat16),
            jax.ShapeDtypeStruct((contexts // PAIR, width, PAIR), jnp.bfloat16),
            jax.ShapeDtypeStruct((width // users, width), jnp.float32),
            jax.ShapeDtypeStruct((width, width), jnp.float32),
        ),
        in_specs=[pl.BlockSpec(memory_space=pltpu.HBM)] * 2,
        out_specs=(VMEM_SPEC,) * 4,
        scratch_shapes=[
            pltpu.VMEM((rows, width), jnp.float32),
            pltpu.VMEM((contexts // step_rows, step_rows, width), jnp.float32),
            pltpu.SemaphoreType.DMA((contexts // step_rows + 1,)),
            pltpu.SemaphoreType.DMA((users // 2 - 1, 2)),
            pltpu.SemaphoreType.DMA((users // 2, 2)),
        ]
        + gram_scratch(users, side, width),
        compiler_params=pltpu.CompilerParams(
            collective_id=0, has_side_effects=True, vmem_limit_bytes=16 * 2**20
        ),
        name="gather_items",
    )(
        pltpu.with_memory_space_constraint(item_factor, pltpu.HBM),
        pltpu.with_memory_space_constraint(context_factor, pltpu.HBM),
    )


def user_kernel(
    axis_sizes, side, partial, gram_rows, context_gram, raw, gathered, raw_gram, arrived, mixed, settled,
    work, far_sems, near_sems, out_sems, on_sems, system_sems, raw_block, raw_sems,
    gram, by_user, by_slow, by_fast, user_sems, slow_sems, fast_sems,
):
    users, items = axis_sizes
    user, item = lax.axis_index("user"), lax.axis_index("item")
    slow, fast, at_slow, at_fast = torus(side)
    half = partial.shape[2] // 2
    blocks = work.shape[0] // BLOCK
    everyone = (("user", users), ("item", items))
    greet(everyone)
    await_greetings(everyone)
    system = blocks_back(gram_rows, work, system_sems, users)

    far = []
    for ahead in HOPS:
        far.append(
            copy_to(
                partial.at[lax.rem(slow + ahead, side), :, pl.ds(0, half)],
                arrived.at[0, ahead - 1],
                far_sems.at[0, ahead - 1],
                user,
                at_slow(ahead),
            )
        )
        far.append(
            copy_to(
                partial.at[:, lax.rem(fast + ahead, side), pl.ds(half, half)],
                arrived.at[1, ahead - 1],
                far_sems.at[1, ahead - 1],
                user,
                at_fast(ahead),
            )
        )
    receive(system)
    work[...] = work[...] * context_gram[...]
    invert(work, 0, SPLIT)

    def combine(part, where):
        own = partial[slow, where, :half] if part == 0 else partial[where, fast, half:]
        total = own.astype(jnp.float32)
        for ahead in range(side - 1):
            total = total + arrived[part, ahead, where].astype(jnp.float32)
        return total

    near = []
    kept = []
    for part in range(2):
        receive(far[part::2])
        here = fast if part == 0 else slow
        for ahead in HOPS:
            where = lax.rem(here + ahead, side)
            mixed[part, ahead - 1] = combine(part, where).astype(mixed.dtype)
            near.append(
                copy_to(
                    mixed.at[part, ahead - 1],
                    settled.at[part, ahead - 1],
                    near_sems.at[part, ahead - 1],
                    user,
                    at_fast(ahead) if part == 0 else at_slow(ahead),
                )
            )
        kept.append(combine(part, here))
    invert(work, SPLIT, blocks)
    receive(near)
    total = jnp.concatenate(
        [
            kept[part] + sum(settled[part, at].astype(jnp.float32) for at in range(side - 1))
            for part in range(2)
        ],
        axis=0,
    )
    raw[...] = dot(total, work[...])
    columns = raw[...].T
    for part in range(2):
        gathered[item, part] = columns[:, part * PAIR : (part + 1) * PAIR].astype(jnp.bfloat16)

    onward = []

    def pass_on(block, part, stage):
        for ahead in HOPS:
            onward.append(
                copy_to(
                    gathered.at[block, part],
                    gathered.at[block, part],
                    on_sems.at[part, stage, ahead - 1],
                    user,
                    at_fast(ahead) if part == 0 else at_slow(ahead),
                )
            )

    outward = []
    for ahead in HOPS:
        for part in range(2):
            outward.append(
                copy_to(
                    gathered.at[item, part],
                    gathered.at[item, part],
                    out_sems.at[part, ahead - 1],
                    user,
                    at_slow(ahead) if part == 0 else at_fast(ahead),
                )
            )
    gram[...] = gram_of(columns)
    first = gram_to_users(gram, by_user, user_sems, users)
    for part in range(2):
        pass_on(item, part, 0)

    def forward(at):
        for part in range(2):
            outward[2 * at + part].wait_recv()
            back = side - HOPS[at]
            pass_on(at_slow(back) if part == 0 else at_fast(back), part, HOPS[at])

    second = exchange(first, by_user, slow, at_slow, by_slow, slow_sems)
    forward(0)
    third = exchange(second, by_slow, fast, at_fast, by_fast, fast_sems)
    forward(1)
    forward(2)
    receive(third)
    raw_block[...] = jnp.sum(by_fast[...], axis=0)
    fourth = blocks_back(raw_block, raw_gram, raw_sems, users)
    receive(onward)
    receive(fourth)
    for copy in system + far + near + outward + onward + first + second + third + fourth:
        copy.wait_send()


def update_users(partial, gram_rows, context_gram, axis_sizes):
    users, items = axis_sizes
    side, _, rows, width = partial.shape
    half = rows // 2
    square = jax.ShapeDtypeStruct((width, width), jnp.float32)
    return pl.pallas_call(
        functools.partial(user_kernel, axis_sizes, side),
        out_shape=(
            jax.ShapeDtypeStruct((rows, width), jnp.float32),
            jax.ShapeDtypeStruct((items, rows // PAIR, width, PAIR), jnp.bfloat16),
            square,
        ),
        in_specs=[VMEM_SPEC] * 3,
        out_specs=(VMEM_SPEC,) * 3,
        scratch_shapes=[
            pltpu.VMEM((2, side - 1, side, half, width), jnp.bfloat16),
            pltpu.VMEM((2, side - 1, half, width), jnp.bfloat16),
            pltpu.VMEM((2, side - 1, half, width), jnp.bfloat16),
            pltpu.VMEM((width, width), jnp.float32),
            pltpu.SemaphoreType.DMA((2, side - 1, 2)),
            pltpu.SemaphoreType.DMA((2, side - 1, 2)),
            pltpu.SemaphoreType.DMA((2, side - 1, 2)),
            pltpu.SemaphoreType.DMA((2, side, side - 1, 2)),
            pltpu.SemaphoreType.DMA((2, users - 1)),
            pltpu.VMEM((width // users, width), jnp.float32),
            pltpu.SemaphoreType.DMA((2, users - 1)),
        ]
        + gram_scratch(users, side, width),
        compiler_params=pltpu.CompilerParams(
            collective_id=1, has_side_effects=True, vmem_limit_bytes=24 * 2**20
        ),
        name="update_users",
    )(partial, gram_rows, context_gram)


def item_kernel(
    axis_sizes, partial, raw_gram, context_gram, raw, new_items, user_factor, arrived, work,
    user_sums, item_sums, user_sems, item_sems, sems
):
    users, items = axis_sizes
    user, item = lax.axis_index("user"), lax.axis_index("item")
    everyone = (("user", users), ("item", items))
    greet(everyone)
    await_greetings(everyone)
    copies = send_all(
        "user",
        users,
        lambda peer, ahead: partial.at[peer],
        lambda me, ahead: arrived.at[ahead - 1],
        sems,
    )
    width = work.shape[0]
    rows_total = jnp.float32(user_factor.shape[0] * users * items)
    down = lax.broadcasted_iota(jnp.int32, (width, width), 0)
    across = lax.broadcasted_iota(jnp.int32, (width, width), 1)
    diagonal = jnp.where(down == across, raw_gram[...], 0.0)
    scale_row = jnp.sqrt(rows_total / (jnp.sum(diagonal, axis=0, keepdims=True) + 1e-06))
    scale_column = jnp.sqrt(rows_total / (jnp.sum(diagonal, axis=1, keepdims=True) + 1e-06))
    user_factor[...] = raw[...] * scale_row
    work[...] = raw_gram[...] * scale_column * scale_row * context_gram[...]
    invert(work, 0, width // BLOCK)
    total = partial[user].astype(jnp.float32)
    for ahead in range(1, users):
        copies[ahead - 1].wait_recv()
        total = total + arrived[ahead - 1].astype(jnp.float32)
    item_raw = dot(total * scale_row, work[...])
    squares = jnp.sum(item_raw * item_raw, axis=0, keepdims=True)
    user_sums[user] = jnp.broadcast_to(squares, user_sums.shape[1:])
    first = send_all(
        "user", users, lambda peer, ahead: user_sums.at[user], lambda me, ahead: user_sums.at[me], user_sems
    )
    receive(first)
    item_sums[item] = jnp.sum(user_sums[...], axis=0)
    second = send_all(
        "item", items, lambda peer, ahead: item_sums.at[item], lambda me, ahead: item_sums.at[me], item_sems
    )
    receive(second)
    squares = jnp.sum(item_sums[...], axis=0)[:1]
    new_items[...] = item_raw * jnp.sqrt(rows_total / (squares + 1e-06))
    for copy in copies + first + second:
        copy.wait_send()


def update_items(partial, raw_gram, context_gram, raw, axis_sizes):
    users, items = axis_sizes
    _, rows, width = partial.shape
    out = jax.ShapeDtypeStruct((rows, width), jnp.float32)
    return pl.pallas_call(
        functools.partial(item_kernel, axis_sizes),
        out_shape=(out, out),
        in_specs=[VMEM_SPEC] * 4,
        out_specs=(VMEM_SPEC,) * 2,
        scratch_shapes=[
            pltpu.VMEM((users - 1, rows, width), jnp.bfloat16),
            pltpu.VMEM((width, width), jnp.float32),
            pltpu.VMEM((users, 8, width), jnp.float32),
            pltpu.VMEM((items, 8, width), jnp.float32),
            pltpu.SemaphoreType.DMA((2, users - 1)),
            pltpu.SemaphoreType.DMA((2, items - 1)),
            pltpu.SemaphoreType.DMA((2, users - 1)),
        ],
        compiler_params=pltpu.CompilerParams(
            collective_id=2, has_side_effects=True, vmem_limit_bytes=16 * 2**20
        ),
        name="update_items",
    )(partial, raw_gram, context_gram, raw)


def local(
    item_factor, context_factor, tile_count, tile_rows, tile_cols, tile_ctx, nz_offsets, nz_values
):
    axis_sizes = (lax.axis_size("user"), lax.axis_size("item"))
    users, items = axis_sizes
    rows, width = item_factor.shape
    side = math.isqrt(items)
    count = tile_count.reshape(1)
    ids = (tile_rows[0, 0], tile_cols[0, 0], tile_ctx[0, 0])
    offsets = nz_offsets[0, 0]
    values = nz_values[0, 0]
    item_pairs, context_pairs, gram_rows, context_gram = gather_items(
        item_factor, context_factor, axis_sizes, side
    )
    partial_users = mttkrp(
        0, count, ids, offsets, values, item_pairs.reshape(-1, width, PAIR), context_pairs,
        items * rows // TILE,
    )
    raw, user_pairs, raw_gram = update_users(
        partial_users.reshape(side, side, rows, width), gram_rows, context_gram, axis_sizes
    )
    partial_items = mttkrp(
        1, count, ids, offsets, values, user_pairs.reshape(-1, width, PAIR), context_pairs,
        users * rows // TILE,
    )
    new_items, user_factor = update_items(
        partial_items.reshape(users, rows, width), raw_gram, context_gram, raw, axis_sizes
    )
    return (user_factor, new_items)


def solution(mesh):
    in_specs = (
        P(("item", "user"), None),
        P(),
        P("user", "item"),
        P("user", "item", None),
        P("user", "item", None),
        P("user", "item", None),
        P("user", "item", None, None, None),
        P("user", "item", None, None),
    )
    out_specs = (P(("user", "item"), None), P(("item", "user"), None))
    return jax.shard_map(local, mesh=mesh, in_specs=in_specs, out_specs=out_specs, check_vma=False)
```

profile of v0, /device:TPU:1, one launch (start us, length us, event | category | flops | bytes accessed | tf_op | source)
XLA Modules:
  0.0 138.3 jit_solution(10850752978100949591)
XLA Ops:
  1.3 0.0 copy-start
  1.3 0.0 copy-start.1
  1.3 0.0 copy-start.2
  1.3 0.0 copy-start.3
  1.3 0.0 copy-start.4
  1.3 21.9 %gather_items.1 = (bf16[8,2,256,128]{3,2,1,0:T(8,128)(2,1)S(1)}, bf16[32,256,128]{2,1,0:T(8,128)(2,1)S(1)}, f32[32,256]{1,0:T(8,128)S(1)}, f32[256,256]{1,0:T(8,128)S(1)}) custom-call(f32[256,256]{1,0:T(8,128)} %item_factor.1, f32[4096,256]{1,0:T(8,128)} %context_factor.1), custom_call_target="tpu_custom_call" | custom-call | tf_op jit(solution)/shard_map/gather_items/pallas_call | solution.py:383
  23.2 0.0 copy-done
  23.2 0.0 copy-done.1
  23.2 0.0 copy-done.2
  23.3 0.0 copy-done.3
  23.3 0.0 copy-done.4
  23.3 20.9 %mttkrp.2 = bf16[64,64,256]{2,1,0:T(8,128)(2,1)S(1)} custom-call(s32[1]{0:T(128)} %bitcast.10.count, s32[128]{0:T(128)S(1)} %bitcast.22, s32[128]{0:T(128)S(1)} %bitcast.20, s32[128]{0:T(128)S(1)} %bitcast.24, s32[3,128,512]{2,1,0:T(8,128)S(1)} %bitcast.14, f32[128,512]{1,0:T(8,128)S(1)} %bitcast.17, bf16[16,256,128]{2,1,0:T(8,128)(2,1)S(1)} %bitcast.19, ...), custom_call_target="tpu_custom_call" | custom-call | tf_op jit(solution)/shard_map/mttkrp/pallas_call | solution.py:105
  44.2 45.6 %update_users.1 = (f32[256,256]{1,0:T(8,128)S(1)}, bf16[16,2,256,128]{3,2,1,0:T(8,128)(2,1)S(1)}, f32[256,256]{1,0:T(8,128)S(1)}) custom-call(bf16[4,4,256,256]{3,2,1,0:T(8,128)(2,1)S(1)} %bitcast.12, f32[32,256]{1,0:T(8,128)S(1)} %get-tuple-element.13.gram_rows, f32[256,256]{1,0:T(8,128)S(1)} %get-tuple-element.14.context_gram), custom_call_target="tpu_custom_call" | custom-call | tf_op jit(solution)/shard_map/update_users/pallas_call | solution.py:545
  89.8 20.8 %mttkrp.3 = bf16[32,64,256]{2,1,0:T(8,128)(2,1)S(1)} custom-call(s32[1]{0:T(128)} %bitcast.11.count, s32[128]{0:T(128)S(1)} %bitcast.21, s32[128]{0:T(128)S(1)} %bitcast.23, s32[128]{0:T(128)S(1)} %bitcast.25, s32[3,128,512]{2,1,0:T(8,128)S(1)} %bitcast.15, f32[128,512]{1,0:T(8,128)S(1)} %bitcast.18, bf16[32,256,128]{2,1,0:T(8,128)(2,1)S(1)} %bitcast.16, ...), custom_call_target="tpu_custom_call" | custom-call | tf_op jit(solution)/shard_map/mttkrp/pallas_call | solution.py:105
  110.7 26.2 %update_items.1 = (f32[256,256]{1,0:T(8,128)S(1)}, f32[256,256]{1,0:T(8,128)S(1)}) custom-call(bf16[8,256,256]{2,1,0:T(8,128)(2,1)S(1)} %bitcast.13, f32[256,256]{1,0:T(8,128)S(1)} %get-tuple-element.16.raw_gram, f32[256,256]{1,0:T(8,128)S(1)} %get-tuple-element.14.context_gram, f32[256,256]{1,0:T(8,128)S(1)} %get-tuple-element.17.raw), custom_call_target="tpu_custom_call" | custom-call | tf_op jit(solution)/shard_map/update_items/pallas_call | solution.py:627
  136.9 0.7 copy.13
  137.6 0.7 copy.14
Async XLA Ops:
  1.3 22.0 %copy-start = (s32[1,1,3,128,512]{4,3,2,1,0:T(8,128)S(1)}, s32[1,1,3,128,512]{4,3,2,1,0:T(8,128)}, u32[]{:S(2)}) copy-start(s32[1,1,3,128,512]{4,3,2,1,0:T(8,128)} %param.14) | copy-start | bytes 2359300
  1.3 22.0 %copy-start.1 = (f32[1,1,128,512]{3,2,1,0:T(8,128)S(1)}, f32[1,1,128,512]{3,2,1,0:T(8,128)}, u32[]{:S(2)}) copy-start(f32[1,1,128,512]{3,2,1,0:T(8,128)} %param.15) | copy-start | bytes 786436
  1.3 22.0 %copy-start.2 = (s32[1,1,128]{2,1,0:T(1,128)S(1)}, s32[1,1,128]{2,1,0:T(1,128)}, u32[]{:S(2)}) copy-start(s32[1,1,128]{2,1,0:T(1,128)} %param.12) | copy-start | bytes 1540
  1.3 22.0 %copy-start.3 = (s32[1,1,128]{2,1,0:T(1,128)S(1)}, s32[1,1,128]{2,1,0:T(1,128)}, u32[]{:S(2)}) copy-start(s32[1,1,128]{2,1,0:T(1,128)} %param.11) | copy-start | bytes 1540
  1.3 22.0 %copy-start.4 = (s32[1,1,128]{2,1,0:T(1,128)S(1)}, s32[1,1,128]{2,1,0:T(1,128)}, u32[]{:S(2)}) copy-start(s32[1,1,128]{2,1,0:T(1,128)} %param.13) | copy-start | bytes 1540
where the time goes:
time: 139 us; the launch traced here: 138 us
  Pallas kernels  135 us (97%)
  local copies, waits for them, and re-layouts  1.43 us (1%)
  between operations  1.4 us (1%)
    pallas_call x1, Pallas kernels, update_users(): pl.pallas_call(functools.partial(user_kernel, axis_sizes, side), out_shap...  45.6 us
    pallas_call x2, Pallas kernels, mttkrp(): pl.pallas_call(functools.partial(mttkrp_kernel, target_at), out_shape=jax...  41.8 us
    pallas_call x1, Pallas kernels, update_items(): pl.pallas_call(functools.partial(item_kernel, axis_sizes), out_shape=(out...  26.2 us
    pallas_call x1, Pallas kernels, gather_items(): pl.pallas_call(functools.partial(gather_kernel, axis_sizes, side, step_ro...  21.9 us

commit v1 on v0

--- a/solution.py
+++ b/solution.py
@@ -10,7 +10,7 @@
 
 TILE = 64
 UNROLL = 32
-PLAN = (3, 2)
+CONTEXT_STEPS = (3, 2)
 PAIR = 2 * TILE
 BLOCK = 64
 SPLIT = 2
@@ -48,8 +48,16 @@
     context,
     out,
     totals,
+    tiles,
 ):
     totals[...] = jnp.zeros_like(totals)
+
+    def unpack(pair, carry):
+        for half in range(2):
+            tiles[2 * pair + half] = source[pair][:, half * TILE : (half + 1) * TILE]
+        return carry
+
+    lax.fori_loop(0, source.shape[0], unpack, 0)
     rank, entries = totals.shape[2], offsets.shape[2]
 
     def one_hot(row, extent):
@@ -78,11 +86,10 @@
         for at in range(UNROLL):
             row = slice(at, at + 1)
             source_id, context_id = source_ids[first + at], context_ids[first + at]
-            source_row = sources[row] + TILE * lax.rem(source_id, 2)
             context_row = contexts[row] + TILE * lax.rem(context_id, 2)
             source_part = jnp.dot(
-                source[lax.div(source_id, 2)],
-                one_hot(source_row, PAIR),
+                tiles[source_id],
+                one_hot(sources[row], TILE),
                 preferred_element_type=jnp.float32,
             )
             context_part = lanes_of(context[lax.div(context_id, 2)], context_row)
@@ -107,7 +114,10 @@
         out_shape=jax.ShapeDtypeStruct(shape, jnp.bfloat16),
         in_specs=[SMEM_SPEC] * 4 + [VMEM_SPEC] * 4,
         out_specs=VMEM_SPEC,
-        scratch_shapes=[pltpu.VMEM(shape, jnp.float32)],
+        scratch_shapes=[
+            pltpu.VMEM(shape, jnp.float32),
+            pltpu.VMEM((2 * source_pairs.shape[0], shape[2], TILE), jnp.bfloat16),
+        ],
         compiler_params=pltpu.CompilerParams(vmem_limit_bytes=24 * 2**20),
         name="mttkrp",
     )(
@@ -360,14 +370,14 @@
         block = items.at[lax.rem(user + users - 2 * HOPS[at], users)]
         forwarded.append(copy_to(block, block, sibling_sems.at[1 + at], sibling, item))
 
-    lax.fori_loop(0, PLAN[0], transform, 0)
+    lax.fori_loop(0, CONTEXT_STEPS[0], transform, 0)
     second = exchange(first, by_user, slow, at_slow, by_slow, slow_sems)
     forward(0)
     forward(1)
-    lax.fori_loop(PLAN[0], PLAN[0] + PLAN[1], transform, 0)
+    lax.fori_loop(CONTEXT_STEPS[0], CONTEXT_STEPS[0] + CONTEXT_STEPS[1], transform, 0)
     third = exchange(second, by_slow, fast, at_fast, by_fast, fast_sems)
     forward(2)
-    lax.fori_loop(PLAN[0] + PLAN[1], steps, transform, 0)
+    lax.fori_loop(CONTEXT_STEPS[0] + CONTEXT_STEPS[1], steps, transform, 0)
     receive(third)
     gram_rows[...] = jnp.sum(by_fast[...], axis=0)
     receive(forwarded)

time: 139 us -> 143 us (1.029)
  Pallas kernels: 135 us -> 140 us
    pallas_call x2, Pallas kernels: 41.8 us -> 26.7 us  [mttkrp(): pl.pallas_call(functools.partial(mttkrp_kernel, target_at), out_shape=jax...]
    pallas_call x1, Pallas kernels: 45.6 us -> 56.3 us  [update_users(): pl.pallas_call(functools.partial(user_kernel, axis_sizes, side), out_shap...]
    pallas_call x1, Pallas kernels: 26.2 us -> 35.6 us  [update_items(): pl.pallas_call(functools.partial(item_kernel, axis_sizes), out_shape=(out...]
where the time goes in v1:
time: 143 us
  Pallas kernels  140 us (98%)
  local copies, waits for them, and re-layouts  1.43 us (1%)
    pallas_call x1, Pallas kernels, update_users(): pl.pallas_call(functools.partial(user_kernel, axis_sizes, side), out_shap...  56.3 us
    pallas_call x1, Pallas kernels, update_items(): pl.pallas_call(functools.partial(item_kernel, axis_sizes), out_shape=(out...  35.6 us
    pallas_call x2, Pallas kernels, mttkrp(): pl.pallas_call(functools.partial(mttkrp_kernel, target_at), out_shape=jax...  26.7 us
    pallas_call x1, Pallas kernels, gather_items(): pl.pallas_call(functools.partial(gather_kernel, axis_sizes, side, step_ro...  21.9 us

profile of v1, /device:TPU:1, one launch (start us, length us, event | category | flops | bytes accessed | tf_op | source)
XLA Modules:
  0.0 143.3 jit_solution(11943823917327913864)
XLA Ops:
  1.3 0.0 copy-start
  1.3 0.0 copy-start.1
  1.3 0.0 copy-start.2
  1.3 0.0 copy-start.3
  1.3 0.0 copy-start.4
  1.3 21.9 %gather_items.1 = (bf16[8,2,256,128]{3,2,1,0:T(8,128)(2,1)S(1)}, bf16[32,256,128]{2,1,0:T(8,128)(2,1)S(1)}, f32[32,256]{1,0:T(8,128)S(1)}, f32[256,256]{1,0:T(8,128)S(1)}) custom-call(f32[256,256]{1,0:T(8,128)} %item_factor.1, f32[4096,256]{1,0:T(8,128)} %context_factor.1), custom_call_target="tpu_custom_call" | custom-call | tf_op jit(solution)/shard_map/gather_items/pallas_call | solution.py:393
  23.2 0.0 copy-done
  23.2 0.0 copy-done.1
  23.2 0.0 copy-done.2
  23.3 0.0 copy-done.3
  23.3 0.0 copy-done.4
  23.3 12.7 %mttkrp.2 = bf16[64,64,256]{2,1,0:T(8,128)(2,1)S(1)} custom-call(s32[1]{0:T(128)} %bitcast.10.count, s32[128]{0:T(128)S(1)} %bitcast.22, s32[128]{0:T(128)S(1)} %bitcast.20, s32[128]{0:T(128)S(1)} %bitcast.24, s32[3,128,512]{2,1,0:T(8,128)S(1)} %bitcast.14, f32[128,512]{1,0:T(8,128)S(1)} %bitcast.17, bf16[16,256,128]{2,1,0:T(8,128)(2,1)S(1)} %bitcast.19, ...), custom_call_target="tpu_custom_call" | custom-call | tf_op jit(solution)/shard_map/mttkrp/pallas_call | solution.py:112
  36.0 56.3 %update_users.1 = (f32[256,256]{1,0:T(8,128)S(1)}, bf16[16,2,256,128]{3,2,1,0:T(8,128)(2,1)S(1)}, f32[256,256]{1,0:T(8,128)S(1)}) custom-call(bf16[4,4,256,256]{3,2,1,0:T(8,128)(2,1)S(1)} %bitcast.12, f32[32,256]{1,0:T(8,128)S(1)} %get-tuple-element.13.gram_rows, f32[256,256]{1,0:T(8,128)S(1)} %get-tuple-element.14.context_gram), custom_call_target="tpu_custom_call" | custom-call | tf_op jit(solution)/shard_map/update_users/pallas_call | solution.py:555
  92.2 14.1 %mttkrp.3 = bf16[32,64,256]{2,1,0:T(8,128)(2,1)S(1)} custom-call(s32[1]{0:T(128)} %bitcast.11.count, s32[128]{0:T(128)S(1)} %bitcast.21, s32[128]{0:T(128)S(1)} %bitcast.23, s32[128]{0:T(128)S(1)} %bitcast.25, s32[3,128,512]{2,1,0:T(8,128)S(1)} %bitcast.15, f32[128,512]{1,0:T(8,128)S(1)} %bitcast.18, bf16[32,256,128]{2,1,0:T(8,128)(2,1)S(1)} %bitcast.16, ...), custom_call_target="tpu_custom_call" | custom-call | tf_op jit(solution)/shard_map/mttkrp/pallas_call | solution.py:112
  106.3 35.6 %update_items.1 = (f32[256,256]{1,0:T(8,128)S(1)}, f32[256,256]{1,0:T(8,128)S(1)}) custom-call(bf16[8,256,256]{2,1,0:T(8,128)(2,1)S(1)} %bitcast.13, f32[256,256]{1,0:T(8,128)S(1)} %get-tuple-element.16.raw_gram, f32[256,256]{1,0:T(8,128)S(1)} %get-tuple-element.14.context_gram, f32[256,256]{1,0:T(8,128)S(1)} %get-tuple-element.17.raw), custom_call_target="tpu_custom_call" | custom-call | tf_op jit(solution)/shard_map/update_items/pallas_call | solution.py:637
  141.9 0.7 copy.13
  142.6 0.7 copy.14
Async XLA Ops:
  1.3 22.0 %copy-start = (s32[1,1,3,128,512]{4,3,2,1,0:T(8,128)S(1)}, s32[1,1,3,128,512]{4,3,2,1,0:T(8,128)}, u32[]{:S(2)}) copy-start(s32[1,1,3,128,512]{4,3,2,1,0:T(8,128)} %param.14) | copy-start | bytes 2359300
  1.3 22.0 %copy-start.1 = (f32[1,1,128,512]{3,2,1,0:T(8,128)S(1)}, f32[1,1,128,512]{3,2,1,0:T(8,128)}, u32[]{:S(2)}) copy-start(f32[1,1,128,512]{3,2,1,0:T(8,128)} %param.15) | copy-start | bytes 786436
  1.3 22.0 %copy-start.2 = (s32[1,1,128]{2,1,0:T(1,128)S(1)}, s32[1,1,128]{2,1,0:T(1,128)}, u32[]{:S(2)}) copy-start(s32[1,1,128]{2,1,0:T(1,128)} %param.12) | copy-start | bytes 1540
  1.3 22.0 %copy-start.3 = (s32[1,1,128]{2,1,0:T(1,128)S(1)}, s32[1,1,128]{2,1,0:T(1,128)}, u32[]{:S(2)}) copy-start(s32[1,1,128]{2,1,0:T(1,128)} %param.11) | copy-start | bytes 1540
  1.3 22.0 %copy-start.4 = (s32[1,1,128]{2,1,0:T(1,128)S(1)}, s32[1,1,128]{2,1,0:T(1,128)}, u32[]{:S(2)}) copy-start(s32[1,1,128]{2,1,0:T(1,128)} %param.13) | copy-start | bytes 1540

commit v2 on v1

--- a/solution.py
+++ b/solution.py
@@ -48,16 +48,8 @@
     context,
     out,
     totals,
-    tiles,
 ):
     totals[...] = jnp.zeros_like(totals)
-
-    def unpack(pair, carry):
-        for half in range(2):
-            tiles[2 * pair + half] = source[pair][:, half * TILE : (half + 1) * TILE]
-        return carry
-
-    lax.fori_loop(0, source.shape[0], unpack, 0)
     rank, entries = totals.shape[2], offsets.shape[2]
 
     def one_hot(row, extent):
@@ -88,7 +80,7 @@
             source_id, context_id = source_ids[first + at], context_ids[first + at]
             context_row = contexts[row] + TILE * lax.rem(context_id, 2)
             source_part = jnp.dot(
-                tiles[source_id],
+                source[source_id],
                 one_hot(sources[row], TILE),
                 preferred_element_type=jnp.float32,
             )
@@ -107,17 +99,39 @@
     out[...] = totals[...].astype(out.dtype)
 
 
+def unpack_kernel(pairs, tiles):
+    def step(at, carry):
+        for pair in range(8):
+            for half in range(2):
+                tiles[16 * at + 2 * pair + half] = pairs[8 * at + pair][
+                    :, half * TILE : (half + 1) * TILE
+                ]
+        return carry
+
+    lax.fori_loop(0, pairs.shape[0] // 8, step, 0)
+
+
+def unpack(pairs):
+    count, rank, _ = pairs.shape
+    return pl.pallas_call(
+        unpack_kernel,
+        out_shape=jax.ShapeDtypeStruct((2 * count, rank, TILE), pairs.dtype),
+        in_specs=[VMEM_SPEC],
+        out_specs=VMEM_SPEC,
+        compiler_params=pltpu.CompilerParams(vmem_limit_bytes=16 * 2**20),
+        name="unpack",
+    )(pairs)
+
+
 def mttkrp(target_at, count, ids, offsets, values, source_pairs, context_pairs, tiles):
     shape = (tiles, TILE, source_pairs.shape[1])
+    source_tiles = unpack(source_pairs)
     return pl.pallas_call(
         functools.partial(mttkrp_kernel, target_at),
         out_shape=jax.ShapeDtypeStruct(shape, jnp.bfloat16),
         in_specs=[SMEM_SPEC] * 4 + [VMEM_SPEC] * 4,
         out_specs=VMEM_SPEC,
-        scratch_shapes=[
-            pltpu.VMEM(shape, jnp.float32),
-            pltpu.VMEM((2 * source_pairs.shape[0], shape[2], TILE), jnp.bfloat16),
-        ],
+        scratch_shapes=[pltpu.VMEM(shape, jnp.float32)],
         compiler_params=pltpu.CompilerParams(vmem_limit_bytes=24 * 2**20),
         name="mttkrp",
     )(
@@ -127,7 +141,7 @@
         ids[2],
         offsets,
         values,
-        source_pairs,
+        source_tiles,
         context_pairs,
     )
 

time: 143 us -> 141 us (0.986)
  Pallas kernels: 140 us -> 137 us
    pallas_call x2, Pallas kernels: 26.7 us -> 41.8 us  [mttkrp(): pl.pallas_call(functools.partial(mttkrp_kernel, target_at), out_shape=jax...]
    pallas_call x1, Pallas kernels: 56.3 us -> 45.9 us  [update_users(): pl.pallas_call(functools.partial(user_kernel, axis_sizes, side), out_shap...]
    pallas_call x1, Pallas kernels: 35.6 us -> 25.5 us  [update_items(): pl.pallas_call(functools.partial(item_kernel, axis_sizes), out_shape=(out...]
    pallas_call x0 -> x2, Pallas kernels: none -> 2.09 us  [unpack(): pl.pallas_call(unpack_kernel, out_shape=jax.ShapeDtypeStruct((2 * count,...]
where the time goes in v2:
time: 141 us; the launch traced here: 140 us
  Pallas kernels  137 us (97%)
  local copies, waits for them, and re-layouts  1.86 us (1%)
    pallas_call x1, Pallas kernels, update_users(): pl.pallas_call(functools.partial(user_kernel, axis_sizes, side), out_shap...  45.9 us
    pallas_call x2, Pallas kernels, mttkrp(): pl.pallas_call(functools.partial(mttkrp_kernel, target_at), out_shape=jax...  41.8 us
    pallas_call x1, Pallas kernels, update_items(): pl.pallas_call(functools.partial(item_kernel, axis_sizes), out_shape=(out...  25.5 us
    pallas_call x1, Pallas kernels, gather_items(): pl.pallas_call(functools.partial(gather_kernel, axis_sizes, side, step_ro...  21.9 us

profile of v2, /device:TPU:1, one launch (start us, length us, event | category | flops | bytes accessed | tf_op | source)
XLA Modules:
  0.0 140.4 jit_solution(204630188470387318)
XLA Ops:
  1.3 21.9 %gather_items.1 = (bf16[8,2,256,128]{3,2,1,0:T(8,128)(2,1)S(1)}, bf16[32,256,128]{2,1,0:T(8,128)(2,1)S(1)}, f32[32,256]{1,0:T(8,128)S(1)}, f32[256,256]{1,0:T(8,128)S(1)}) custom-call(f32[256,256]{1,0:T(8,128)} %item_factor.1, f32[4096,256]{1,0:T(8,128)} %context_factor.1), custom_call_target="tpu_custom_call" | custom-call | tf_op jit(solution)/shard_map/gather_items/pallas_call | solution.py:407
  23.2 0.0 copy-start
  23.2 0.0 copy-start.1
  23.2 0.0 copy-start.2
  23.2 0.0 copy-start.3
  23.2 0.0 copy-start.4
  23.2 0.7 unpack.2.source
  23.9 0.4 copy-done
  24.3 0.1 copy-done.1
  24.4 0.0 copy-done.2
  24.4 0.0 copy-done.3
  24.4 0.0 copy-done.4
  24.4 20.9 %mttkrp.2 = bf16[64,64,256]{2,1,0:T(8,128)(2,1)S(1)} custom-call(s32[1]{0:T(128)} %bitcast.10.count, s32[128]{0:T(128)S(1)} %bitcast.22, s32[128]{0:T(128)S(1)} %bitcast.20, s32[128]{0:T(128)S(1)} %bitcast.24, s32[3,128,512]{2,1,0:T(8,128)S(1)} %bitcast.14, f32[128,512]{1,0:T(8,128)S(1)} %bitcast.18, bf16[32,256,64]{2,1,0:T(8,128)(2,1)S(1)} %unpack.2.source, ...), custom_call_target="tpu_custom_call" | custom-call | tf_op jit(solution)/shard_map/mttkrp/pallas_call | solution.py:129
  45.3 45.9 %update_users.1 = (f32[256,256]{1,0:T(8,128)S(1)}, bf16[16,2,256,128]{3,2,1,0:T(8,128)(2,1)S(1)}, f32[256,256]{1,0:T(8,128)S(1)}) custom-call(bf16[4,4,256,256]{3,2,1,0:T(8,128)(2,1)S(1)} %bitcast.12, f32[32,256]{1,0:T(8,128)S(1)} %get-tuple-element.13.gram_rows, f32[256,256]{1,0:T(8,128)S(1)} %get-tuple-element.14.context_gram), custom_call_target="tpu_custom_call" | custom-call | tf_op jit(solution)/shard_map/update_users/pallas_call | solution.py:569
  91.2 1.4 unpack.3.source
  92.6 20.9 %mttkrp.3 = bf16[32,64,256]{2,1,0:T(8,128)(2,1)S(1)} custom-call(s32[1]{0:T(128)} %bitcast.11.count, s32[128]{0:T(128)S(1)} %bitcast.21, s32[128]{0:T(128)S(1)} %bitcast.23, s32[128]{0:T(128)S(1)} %bitcast.25, s32[3,128,512]{2,1,0:T(8,128)S(1)} %bitcast.15, f32[128,512]{1,0:T(8,128)S(1)} %bitcast.19, bf16[64,256,64]{2,1,0:T(8,128)(2,1)S(1)} %unpack.3.source, ...), custom_call_target="tpu_custom_call" | custom-call | tf_op jit(solution)/shard_map/mttkrp/pallas_call | solution.py:129
  113.5 25.5 %update_items.1 = (f32[256,256]{1,0:T(8,128)S(1)}, f32[256,256]{1,0:T(8,128)S(1)}) custom-call(bf16[8,256,256]{2,1,0:T(8,128)(2,1)S(1)} %bitcast.13, f32[256,256]{1,0:T(8,128)S(1)} %get-tuple-element.16.raw_gram, f32[256,256]{1,0:T(8,128)S(1)} %get-tuple-element.14.context_gram, f32[256,256]{1,0:T(8,128)S(1)} %get-tuple-element.17.raw), custom_call_target="tpu_custom_call" | custom-call | tf_op jit(solution)/shard_map/update_items/pallas_call | solution.py:651
  139.0 0.7 copy.13
  139.7 0.7 copy.14
Async XLA Ops:
  23.2 1.1 copy-start
  23.2 1.2 copy-start.1
  23.2 1.2 copy-start.2
  23.2 1.2 copy-start.3
  23.2 1.1 copy-start.4

commit v3 on v0

--- a/solution.py
+++ b/solution.py
@@ -10,7 +10,7 @@
 
 TILE = 64
 UNROLL = 32
-PLAN = (3, 2)
+CONTEXT_STEPS = (3, 2)
 PAIR = 2 * TILE
 BLOCK = 64
 SPLIT = 2
@@ -360,14 +360,14 @@
         block = items.at[lax.rem(user + users - 2 * HOPS[at], users)]
         forwarded.append(copy_to(block, block, sibling_sems.at[1 + at], sibling, item))
 
-    lax.fori_loop(0, PLAN[0], transform, 0)
+    lax.fori_loop(0, CONTEXT_STEPS[0], transform, 0)
     second = exchange(first, by_user, slow, at_slow, by_slow, slow_sems)
     forward(0)
     forward(1)
-    lax.fori_loop(PLAN[0], PLAN[0] + PLAN[1], transform, 0)
+    lax.fori_loop(CONTEXT_STEPS[0], CONTEXT_STEPS[0] + CONTEXT_STEPS[1], transform, 0)
     third = exchange(second, by_slow, fast, at_fast, by_fast, fast_sems)
     forward(2)
-    lax.fori_loop(PLAN[0] + PLAN[1], steps, transform, 0)
+    lax.fori_loop(CONTEXT_STEPS[0] + CONTEXT_STEPS[1], steps, transform, 0)
     receive(third)
     gram_rows[...] = jnp.sum(by_fast[...], axis=0)
     receive(forwarded)
@@ -473,19 +473,24 @@
             )
         kept.append(combine(part, here))
     invert(work, SPLIT, blocks)
-    receive(near)
-    total = jnp.concatenate(
-        [
-            kept[part] + sum(settled[part, at].astype(jnp.float32) for at in range(side - 1))
-            for part in range(2)
-        ],
-        axis=0,
-    )
-    raw[...] = dot(total, work[...])
-    columns = raw[...].T
+    outward = {}
     for part in range(2):
-        gathered[item, part] = columns[:, part * PAIR : (part + 1) * PAIR].astype(jnp.bfloat16)
-
+        receive(near[part * len(HOPS) : (part + 1) * len(HOPS)])
+        total = kept[part]
+        for at in range(side - 1):
+            total = total + settled[part, at].astype(jnp.float32)
+        rows = dot(total, work[...])
+        raw[part * half : (part + 1) * half, :] = rows
+        gathered[item, part] = rows.T.astype(jnp.bfloat16)
+        for ahead in HOPS:
+            outward[part, ahead] = copy_to(
+                gathered.at[item, part],
+                gathered.at[item, part],
+                out_sems.at[part, ahead - 1],
+                user,
+                at_slow(ahead) if part == 0 else at_fast(ahead),
+            )
+    gram[...] = gram_of(raw[...].T)
     onward = []
 
     def pass_on(block, part, stage):
@@ -500,26 +505,13 @@
                 )
             )
 
-    outward = []
-    for ahead in HOPS:
-        for part in range(2):
-            outward.append(
-                copy_to(
-                    gathered.at[item, part],
-                    gathered.at[item, part],
-                    out_sems.at[part, ahead - 1],
-                    user,
-                    at_slow(ahead) if part == 0 else at_fast(ahead),
-                )
-            )
-    gram[...] = gram_of(columns)
     first = gram_to_users(gram, by_user, user_sems, users)
     for part in range(2):
         pass_on(item, part, 0)
 
     def forward(at):
         for part in range(2):
-            outward[2 * at + part].wait_recv()
+            outward[part, HOPS[at]].wait_recv()
             back = side - HOPS[at]
             pass_on(at_slow(back) if part == 0 else at_fast(back), part, HOPS[at])
 
@@ -533,7 +525,7 @@
     fourth = blocks_back(raw_block, raw_gram, raw_sems, users)
     receive(onward)
     receive(fourth)
-    for copy in system + far + near + outward + onward + first + second + third + fourth:
+    for copy in system + far + near + list(outward.values()) + onward + first + second + third + fourth:
         copy.wait_send()
 
 

time: 139 us -> 138 us (level)
    pallas_call x2, Pallas kernels: 41.8 us -> 12.1 us  [mttkrp(): pl.pallas_call(functools.partial(mttkrp_kernel, target_at), out_shape=jax...]
    pallas_call x1, Pallas kernels: 45.6 us -> 61.2 us  [update_users(): pl.pallas_call(functools.partial(user_kernel, axis_sizes, side), out_shap...]
    pallas_call x1, Pallas kernels: 26.2 us -> 40.1 us  [update_items(): pl.pallas_call(functools.partial(item_kernel, axis_sizes), out_shape=(out...]
where the time goes in v3:
time: 138 us
  Pallas kernels  135 us (98%)
  local copies, waits for them, and re-layouts  1.43 us (1%)
  between operations  1.4 us (1%)
    pallas_call x1, Pallas kernels, update_users(): pl.pallas_call(functools.partial(user_kernel, axis_sizes, side), out_shap...  61.2 us
    pallas_call x1, Pallas kernels, update_items(): pl.pallas_call(functools.partial(item_kernel, axis_sizes), out_shape=(out...  40.1 us
    pallas_call x1, Pallas kernels, gather_items(): pl.pallas_call(functools.partial(gather_kernel, axis_sizes, side, step_ro...  21.9 us
    pallas_call x2, Pallas kernels, mttkrp(): pl.pallas_call(functools.partial(mttkrp_kernel, target_at), out_shape=jax...  12.1 us

profile of v3, /device:TPU:1, one launch (start us, length us, event | category | flops | bytes accessed | tf_op | source)
XLA Modules:
  0.0 138.1 jit_solution(8470551539150032540)
XLA Ops:
  1.3 0.0 copy-start
  1.3 0.0 copy-start.1
  1.3 0.0 copy-start.2
  1.3 0.0 copy-start.3
  1.3 0.0 copy-start.4
  1.3 21.9 %gather_items.1 = (bf16[8,2,256,128]{3,2,1,0:T(8,128)(2,1)S(1)}, bf16[32,256,128]{2,1,0:T(8,128)(2,1)S(1)}, f32[32,256]{1,0:T(8,128)S(1)}, f32[256,256]{1,0:T(8,128)S(1)}) custom-call(f32[256,256]{1,0:T(8,128)} %item_factor.1, f32[4096,256]{1,0:T(8,128)} %context_factor.1), custom_call_target="tpu_custom_call" | custom-call | tf_op jit(solution)/shard_map/gather_items/pallas_call | solution.py:383
  23.2 0.0 copy-done
  23.2 0.0 copy-done.1
  23.2 0.0 copy-done.2
  23.3 0.0 copy-done.3
  23.3 0.0 copy-done.4
  23.3 6.1 %mttkrp.2 = bf16[64,64,256]{2,1,0:T(8,128)(2,1)S(1)} custom-call(s32[1]{0:T(128)} %bitcast.10.count, s32[128]{0:T(128)S(1)} %bitcast.22, s32[128]{0:T(128)S(1)} %bitcast.20, s32[128]{0:T(128)S(1)} %bitcast.24, s32[3,128,512]{2,1,0:T(8,128)S(1)} %bitcast.14, f32[128,512]{1,0:T(8,128)S(1)} %bitcast.17, bf16[16,256,128]{2,1,0:T(8,128)(2,1)S(1)} %bitcast.19, ...), custom_call_target="tpu_custom_call" | custom-call | tf_op jit(solution)/shard_map/mttkrp/pallas_call | solution.py:105
  29.4 61.2 %update_users.1 = (f32[256,256]{1,0:T(8,128)S(1)}, bf16[16,2,256,128]{3,2,1,0:T(8,128)(2,1)S(1)}, f32[256,256]{1,0:T(8,128)S(1)}) custom-call(bf16[4,4,256,256]{3,2,1,0:T(8,128)(2,1)S(1)} %bitcast.12, f32[32,256]{1,0:T(8,128)S(1)} %get-tuple-element.13.gram_rows, f32[256,256]{1,0:T(8,128)S(1)} %get-tuple-element.14.context_gram), custom_call_target="tpu_custom_call" | custom-call | tf_op jit(solution)/shard_map/update_users/pallas_call | solution.py:537
  90.6 6.0 %mttkrp.3 = bf16[32,64,256]{2,1,0:T(8,128)(2,1)S(1)} custom-call(s32[1]{0:T(128)} %bitcast.11.count, s32[128]{0:T(128)S(1)} %bitcast.21, s32[128]{0:T(128)S(1)} %bitcast.23, s32[128]{0:T(128)S(1)} %bitcast.25, s32[3,128,512]{2,1,0:T(8,128)S(1)} %bitcast.15, f32[128,512]{1,0:T(8,128)S(1)} %bitcast.18, bf16[32,256,128]{2,1,0:T(8,128)(2,1)S(1)} %bitcast.16, ...), custom_call_target="tpu_custom_call" | custom-call | tf_op jit(solution)/shard_map/mttkrp/pallas_call | solution.py:105
  96.6 40.1 %update_items.1 = (f32[256,256]{1,0:T(8,128)S(1)}, f32[256,256]{1,0:T(8,128)S(1)}) custom-call(bf16[8,256,256]{2,1,0:T(8,128)(2,1)S(1)} %bitcast.13, f32[256,256]{1,0:T(8,128)S(1)} %get-tuple-element.16.raw_gram, f32[256,256]{1,0:T(8,128)S(1)} %get-tuple-element.14.context_gram, f32[256,256]{1,0:T(8,128)S(1)} %get-tuple-element.17.raw), custom_call_target="tpu_custom_call" | custom-call | tf_op jit(solution)/shard_map/update_items/pallas_call | solution.py:619
  136.7 0.7 copy.13
  137.4 0.7 copy.14
Async XLA Ops:
  1.3 22.0 %copy-start = (s32[1,1,3,128,512]{4,3,2,1,0:T(8,128)S(1)}, s32[1,1,3,128,512]{4,3,2,1,0:T(8,128)}, u32[]{:S(2)}) copy-start(s32[1,1,3,128,512]{4,3,2,1,0:T(8,128)} %param.14) | copy-start | bytes 2359300
  1.3 22.0 %copy-start.1 = (f32[1,1,128,512]{3,2,1,0:T(8,128)S(1)}, f32[1,1,128,512]{3,2,1,0:T(8,128)}, u32[]{:S(2)}) copy-start(f32[1,1,128,512]{3,2,1,0:T(8,128)} %param.15) | copy-start | bytes 786436
  1.3 22.0 %copy-start.2 = (s32[1,1,128]{2,1,0:T(1,128)S(1)}, s32[1,1,128]{2,1,0:T(1,128)}, u32[]{:S(2)}) copy-start(s32[1,1,128]{2,1,0:T(1,128)} %param.12) | copy-start | bytes 1540
  1.3 22.0 %copy-start.3 = (s32[1,1,128]{2,1,0:T(1,128)S(1)}, s32[1,1,128]{2,1,0:T(1,128)}, u32[]{:S(2)}) copy-start(s32[1,1,128]{2,1,0:T(1,128)} %param.11) | copy-start | bytes 1540
  1.3 22.0 %copy-start.4 = (s32[1,1,128]{2,1,0:T(1,128)S(1)}, s32[1,1,128]{2,1,0:T(1,128)}, u32[]{:S(2)}) copy-start(s32[1,1,128]{2,1,0:T(1,128)} %param.13) | copy-start | bytes 1540
